TPU v7x, 1024 devices: a whole 8x8x8 slice. The times are simulated.
1024 devices in a mesh: seq: 64 (over y, x), head: 16 (over z, core).
Axes of the slice: x: 8, y: 8, z: 8, core: 2. Of those that a mesh axis runs over, the one named last changes fastest.
Arguments:
- lin_qkv: bfloat16 [16384, 3, 4096], P('seq', None, 'head'), may hold values from -6 to 6
- resid: bfloat16 [16384, 4096], P('seq', 'head'), may hold values from -6 to 6
- w_out: bfloat16 [4096, 4096], P('head'), may hold values from -0.125 to 0.125
- w_qkv: bfloat16 [4096, 3, 4096], P(None, None, 'head'), may hold values from -2 to 2
Outputs:
- hidden: bfloat16 [16384, 4096], P('seq', 'head')
- attended: bfloat16 [16384, 4096], P('seq', 'head')
All inputs are finite; a program needn't handle non-finite values.
Results may differ from a plain program's by a relative error of at most 0.025.
Values may be sent and summed in bfloat16 or wider, within the bound.
A program may use at most 64 MiB of HBM per device.

v0:
```python
import math

import jax
import jax.numpy as jnp
from jax import lax
from jax.sharding import Mesh
from jax.sharding import PartitionSpec as P

D = 4096
HD = 128
SEQ = ("seq_0", "seq_1")


def nothing_yet(array, identity):
    return jnp.zeros_like(array) + jnp.asarray(identity, array.dtype)


def entering(array, axes, combine, identity):
    before = start = nothing_yet(array, identity)
    so_far = array
    for axis in reversed(axes):
        devices, here = (lax.axis_size(axis), lax.axis_index(axis))
        pieces = lax.all_gather(so_far, axis)
        inside, so_far = (start, start)
        for k in range(devices):
            passed = k < here
            so_far = combine(so_far, pieces[k])
            inside = jnp.where(passed, so_far, inside)
        before = combine(inside, before)
    return before


def laid_out(blocks, dim):
    lengths = list(blocks.shape[1:])
    lengths[dim] *= blocks.shape[0]
    return jnp.moveaxis(blocks, 0, dim).reshape(lengths)


def from_everyone(array, axis):
    devices = lax.axis_size(axis)
    return lax.all_to_all(
        jnp.broadcast_to(array[None], (devices, *array.shape)), axis, 0, 0, tiled=True
    )


def gather_directly(array, axis, dim):
    return laid_out(from_everyone(array, axis), dim)


def shifted(array, axis, by):
    devices = lax.axis_size(axis)
    pairs = [(i, i + by) for i in range(devices) if 0 <= i + by < devices]
    return lax.ppermute(array, axis, pairs)


def rotary(values, positions):
    half = values.shape[-1] // 2
    freq = 500000.0 ** (-(jnp.arange(half, dtype=jnp.float32) * 2.0 / values.shape[-1]))
    angle = positions.astype(jnp.float32)[:, None] * freq[None, :]
    cosine = jnp.cos(angle)[:, None, :]
    sine = jnp.sin(angle)[:, None, :]
    first = values[..., :half]
    second = values[..., half:]
    return jnp.concatenate(
        [first * cosine - second * sine, second * cosine + first * sine], axis=-1
    )


def add_states(earlier, later):
    return earlier + later


def local(lin_qkv, resid, w_out, w_qkv):
    tok_rows = lin_qkv.shape[0]
    local_width = lin_qkv.shape[2]
    nheads = local_width // HD
    n_seq = lax.axis_size(SEQ)
    own_index = lax.axis_index(SEQ)
    queries = lin_qkv[:, 0].reshape(tok_rows, nheads, HD)
    keys = lin_qkv[:, 1].reshape(tok_rows, nheads, HD)
    values = lin_qkv[:, 2].reshape(tok_rows, nheads, HD)
    weight_cols = lax.all_to_all(w_out, "head", split_axis=1, concat_axis=0, tiled=True)
    own_state = jnp.einsum("thd,the->hde", keys, values, preferred_element_type=jnp.float32)
    before = entering(own_state, SEQ, add_states, jnp.zeros_like(own_state))
    before = before.astype(jnp.bfloat16)
    causal = jnp.tril(jnp.ones((tok_rows, tok_rows), dtype=bool))
    scores = jnp.einsum("thd,shd->hts", queries, keys, preferred_element_type=jnp.float32)
    inner = jnp.where(causal[None], scores, 0.0).astype(jnp.bfloat16)
    total = jnp.einsum("hts,shd->thd", inner, values, preferred_element_type=jnp.float32)
    total = total + jnp.einsum("thd,hde->the", queries, before, preferred_element_type=jnp.float32)
    scale = 1.0 / math.sqrt(HD * tok_rows * n_seq)
    lin_out = (total * scale).astype(jnp.bfloat16).reshape(tok_rows, local_width)
    shared = jnp.dot(
        gather_directly(lin_out, "head", 1), weight_cols, preferred_element_type=jnp.float32
    )
    mixed_f = resid.astype(jnp.float32) + shared
    hidden = mixed_f.astype(jnp.bfloat16)
    flat_w = w_qkv.reshape(w_qkv.shape[0], 3 * local_width)
    whole = lax.all_gather(mixed_f, "head", axis=1, tiled=True)
    meansq = jnp.sum(whole * whole, axis=1, keepdims=True) / D
    normed = (whole * lax.rsqrt(meansq + 1e-05)).astype(jnp.bfloat16)
    proj = jnp.dot(normed, flat_w, preferred_element_type=jnp.float32)
    proj = proj.reshape(tok_rows, 3, nheads, HD)
    positions = own_index * tok_rows + jnp.arange(tok_rows, dtype=jnp.int32)
    query2 = rotary(proj[:, 0], positions).astype(jnp.bfloat16)
    key2 = rotary(proj[:, 1], positions).astype(jnp.bfloat16)
    value2 = proj[:, 2].astype(jnp.bfloat16)
    key_prev, value_prev = shifted((key2, value2), SEQ, 1)
    score_scale = 1.0 / math.sqrt(HD)
    all_keys = jnp.concatenate([key_prev, key2], axis=0)
    all_values = jnp.concatenate([value_prev, value2], axis=0)
    logits = (
        jnp.einsum("thd,shd->hts", query2, all_keys, preferred_element_type=jnp.float32)
        * score_scale
    )
    allowed = jnp.concatenate([jnp.full((tok_rows, tok_rows), own_index > 0), causal], axis=1)
    logits = jnp.where(allowed[None], logits, -1e30)
    top = jnp.max(logits, axis=2, keepdims=True)
    expo = jnp.where(allowed[None], jnp.exp(logits - top), 0.0)
    weights = (expo / jnp.sum(expo, axis=2, keepdims=True)).astype(jnp.bfloat16)
    attended = jnp.einsum("hts,shd->thd", weights, all_values, preferred_element_type=jnp.float32)
    return (hidden, attended.astype(jnp.bfloat16).reshape(tok_rows, local_width))


def solution(mesh):
    finer = Mesh(mesh.devices.reshape(8, 8, mesh.shape["head"]), ("seq_0", "seq_1", "head"))
    placed = (P(SEQ, None, "head"), P(SEQ, "head"), P("head", None), P(None, None, "head"))
    return jax.shard_map(
        local,
        mesh=finer,
        in_specs=placed,
        out_specs=(P(SEQ, "head"), P(SEQ, "head")),
        check_vma=False,
    )
```

profile of v0, /device:TPU:1, one launch (start us, length us, event | category | flops | bytes accessed | tf_op | source)
XLA Modules:
  0.0 245.7 jit_solution(17669746644643604411)
XLA Ops:
  7.2 1.1 fusion.81
  8.5 0.8 fusion.88
  9.4 3.3 %copy.50 = bf16[256,4096]{0,1:T(8,128)(2,1)S(1)} copy(bf16[256,4096]{1,0:T(8,128)(2,1)} %param.6) | data formatting | bytes 4194304 | tf_op args[2]
  12.6 2.4 copy.51
  15.0 18.2 %all-to-all-start.1 = ((bf16[256,16,256]{2,0,1:T(8,128)(2,1)}), bf16[256,16,256]{2,0,1:T(8,128)(2,1)S(1)}, u32[]{:S(2)}, u32[]{:S(2)}) async-start(bf16[256,16,256]{2,0,1:T(8,128)(2,1)} %copy.51), calls=%async_computation.1 | async-start | bytes 4194304 | tf_op jit(solution)/shard_map/all_to_all | solution.py:82
  33.3 29.5 %all-gather.9.cloned.1.call-done = f32[16,128,128]{2,1,0:T(8,128)} async-done(((f32[2,128,128]{2,1,0:T(8,128)}), f32[16,128,128]{2,1,0:T(8,128)}) %all-gather.9.cloned.1.call-update) | async-done | bytes 1048592 | tf_op jit(solution)/shard_map/all_gather | solution.py:23
  62.8 2.0 fusion.42
  65.1 43.8 %all-gather.5.cloned.1.call-done = f32[8,2,128,128]{3,2,1,0:T(8,128)} async-done(((f32[1,2,128,128]{3,2,1,0:T(8,128)}), f32[8,2,128,128]{3,2,1,0:T(8,128)}) %all-gather.5.cloned.1.call-update) | async-done | bytes 1048592 | tf_op jit(solution)/shard_map/all_gather | solution.py:23
  108.9 1.9 convolution_bitcast_fusion
  110.8 0.4 fusion.27
  111.6 64.6 %all_to_all.21 = bf16[16,256,256]{2,1,0:T(8,128)(2,1)S(1)} all-to-all(bf16[16,256,256]{2,1,0:T(8,128)(2,1)S(1)} %broadcast_in_dim.62), channel_id=1, replica_groups=mesh['seq_0'=8,'seq_1'=8,'head'=16] {'head'}, dimensions={0} | all-to-all | bytes 4194304 | tf_op jit(solution)/shard_map/all_to_all | solution.py:41
  176.2 1.5 fusion.82
  177.6 8.8 %copy.52 = bf16[4096,3,256]{0,2,1:T(8,128)(2,1)} copy(bf16[4096,3,256]{2,0,1:T(8,128)(2,1)} %param.7) | data formatting | bytes 12582912 | tf_op args[3]
  186.4 0.3 multiply_cosine_fusion
  186.8 34.5 %all-gather.7.cloned.1.call-done = f32[256,4096]{1,0:T(8,128)} async-done(((f32[256,256]{1,0:T(8,128)}), f32[256,4096]{1,0:T(8,128)}) %all-gather.7.cloned.1.call-update) | async-done | bytes 4194320 | tf_op jit(solution)/shard_map/all_gather | solution.py:99
  221.2 2.7 %multiply_reduce_fusion = f32[256]{0:T(256)S(1)} fusion(f32[256,4096]{1,0:T(8,128)} %all-gather.7.cloned.1.call-done), kind=kLoop, calls=%fused_computation.2 | loop fusion | flops 2096896 | bytes 4195328 | tf_op jit(solution)/shard_map/reduce_sum | solution.py:100
  224.0 0.7 copy-done
  224.7 4.7 %fusion.2 = f32[256,3,2,128]{0,3,2,1:T(8,128)S(1)} fusion(bf16[3,2,128,4096]{3,2,1,0:T(8,128)(2,1)} %bitcast.76, f32[256,4096]{1,0:T(8,128)S(1)} %copy-done, f32[256]{0:T(256)S(1)} %add_rsqrt_fusion), kind=kOutput, calls=%fused_computation.4 | convolution fusion | flops 1612709888 | bytes 11273216 | tf_op jit(solution)/shard_map/dot_general | solution.py:102
  229.5 3.1 %collective-permute-start.1 = (bf16[256,2,128]{0,2,1:T(8,128)(2,1)S(1)}, bf16[256,2,128]{0,2,1:T(8,128)(2,1)S(1)}, u32[]{:S(2)}, u32[]{:S(2)}) collective-permute-start(bf16[256,2,128]{0,2,1:T(8,128)(2,1)S(1)} %pad_maximum_fusion), channel_id=1, source_target_pairs={{0,16},{16,32},{32,48},{48,64},{64,80},{80,96},{96,112},{112,128},... | collective-permute-start | bytes 393224 | tf_op jit(solution)/shard_map/ppermute | solution.py:53
  232.7 3.1 %collective-permute-start = (bf16[256,2,128]{0,2,1:T(8,128)(2,1)S(1)}, bf16[256,2,128]{0,2,1:T(8,128)(2,1)S(1)}, u32[]{:S(2)}, u32[]{:S(2)}) collective-permute-start(bf16[256,2,128]{0,2,1:T(8,128)(2,1)S(1)} %fusion.38), channel_id=1, source_target_pairs={{0,16},{16,32},{32,48},{48,64},{64,80},{80,96},{96,112},{112,128},... | collective-permute-start | bytes 393224 | tf_op jit(solution)/shard_map/ppermute | solution.py:53
  235.8 0.7 fusion.83
  236.5 1.6 collective-permute-done
  238.0 0.4 convolution_convert_fusion
  238.4 0.8 copy.55
  (25 shorter events, 1.0 us)
Async XLA Ops:
  7.2 55.7 %all-gather.9.cloned.1.call-start = ((), (), s32[]{:S(2)}) async-start(), calls=%async_computation.4 | async-start | bytes 1179648 | tf_op jit(solution)/shard_map/all_gather | solution.py:23
  15.0 96.3 %all-to-all-start.1 = ((bf16[256,16,256]{2,0,1:T(8,128)(2,1)}), bf16[256,16,256]{2,0,1:T(8,128)(2,1)S(1)}, u32[]{:S(2)}, u32[]{:S(2)}) async-start(bf16[256,16,256]{2,0,1:T(8,128)(2,1)} %copy.51), calls=%async_computation.1 | async-start | bytes 4194304 | tf_op jit(solution)/shard_map/all_to_all | solution.py:82
  33.2 75.7 %all-gather.5.cloned.1.call-start = ((), (), s32[]{:S(2)}) async-start(), calls=%async_computation.2 | async-start | bytes 1179648 | tf_op jit(solution)/shard_map/all_gather | solution.py:23
  64.8 156.4 %all-gather.7.cloned.1.call-start = ((), (), s32[]{:S(2)}) async-start(), calls=%async_computation.3 | async-start | bytes 4456448 | tf_op jit(solution)/shard_map/all_gather | solution.py:99
  111.5 64.6 %copy-start.1 = (bf16[256,256]{1,0:T(8,128)(2,1)S(1)}, bf16[256,256]{1,0:T(8,128)(2,1)}, u32[]{:S(2)}) copy-start(bf16[256,256]{1,0:T(8,128)(2,1)} %param.5) | copy-start | bytes 393220
  221.2 3.4 %copy-start = (f32[256,4096]{1,0:T(8,128)S(1)}, f32[256,4096]{1,0:T(8,128)}, u32[]{:S(2)}) copy-start(f32[256,4096]{1,0:T(8,128)} %all-gather.7.cloned.1.call-done) | copy-start | bytes 12582916
  229.5 6.2 %collective-permute-start.1 = (bf16[256,2,128]{0,2,1:T(8,128)(2,1)S(1)}, bf16[256,2,128]{0,2,1:T(8,128)(2,1)S(1)}, u32[]{:S(2)}, u32[]{:S(2)}) collective-permute-start(bf16[256,2,128]{0,2,1:T(8,128)(2,1)S(1)} %pad_maximum_fusion), channel_id=1, source_target_pairs={{0,16},{16,32},{32,48},{48,64},{64,80},{80,96},{96,112},{112,128},... | collective-permute-start | bytes 393224 | tf_op jit(solution)/shard_map/ppermute | solution.py:53
  232.7 5.4 %collective-permute-start = (bf16[256,2,128]{0,2,1:T(8,128)(2,1)S(1)}, bf16[256,2,128]{0,2,1:T(8,128)(2,1)S(1)}, u32[]{:S(2)}, u32[]{:S(2)}) collective-permute-start(bf16[256,2,128]{0,2,1:T(8,128)(2,1)S(1)} %fusion.38), channel_id=1, source_target_pairs={{0,16},{16,32},{32,48},{48,64},{64,80},{80,96},{96,112},{112,128},... | collective-permute-start | bytes 393224 | tf_op jit(solution)/shard_map/ppermute | solution.py:53
Sparse Core Ops, SparseCore 0:
  11.2 51.5 all-gather.8
  66.1 42.7 all-gather.4
  177.7 43.4 all-gather.6
where the time goes:
time: 250 us; the launch traced here: 246 us
  waiting for transfers between devices  109 us (44%)
  blocking collectives  64.6 us (26%)
  starting transfers between devices  24.5 us (10%)
  local copies, waits for them, and re-layouts  17.7 us (7%)
  between operations  14 us (6%)
  matrix products  10.4 us (4%)
  other arithmetic  5.13 us (2%)
    all_gather x2, waiting for transfers between devices, entering(): pieces = lax.all_gather(so_far, axis)  73.4 us
    all_to_all x1, blocking collectives, from_everyone(): lax.all_to_all(jnp.broadcast_to(array[None], (devices, *array.shape)), ax...  64.6 us
    all_gather x1, waiting for transfers between devices, local(): whole = lax.all_gather(mixed_f, 'head', axis=1, tiled=True)  34.5 us
    all_to_all x1, starting transfers between devices, local(): lax.all_to_all(w_out, 'head', split_axis=1, concat_axis=0, tiled=True)  18.2 us
    unnamed x9, local copies, waits for them, and re-layouts  13.7 us
    ppermute x2, starting transfers between devices, shifted(): return lax.ppermute(array, axis, pairs)  6.19 us
  transfers between devices with their start and end apart: 6, of which 4 were waited for; matrix products, arithmetic and copies ran while one was open for 8% of the time, Pallas kernels for 0%

commit v1 on v0

v1 whole, which is shorter than its diff:
```python
import functools
import math

import jax
import jax.numpy as jnp
import numpy as np
from jax import lax
from jax.experimental import pallas as pl
from jax.experimental.pallas import tpu as pltpu
from jax.sharding import Mesh
from jax.sharding import PartitionSpec as P

HD = 128
BF = jnp.bfloat16
F32 = jnp.float32
MESH_ID = pl.DeviceIdType.MESH


def dot(a, b, contract=(1, 0)):
    dims = (((contract[0],), (contract[1],)), ((), ()))
    return lax.dot_general(a, b, dims, preferred_element_type=F32)


def remote(src, dst, send, recv, **where):
    return pltpu.make_async_remote_copy(
        src_ref=src, dst_ref=dst, send_sem=send, recv_sem=recv, device_id=where, device_id_type=MESH_ID
    )


def far_first(n):
    return sorted(range(1, n), key=lambda k: -min(k, n - k))


def layer_pair(
    sizes,
    scale,
    qkv_hbm,
    resid_hbm,
    wo_hbm,
    wq_hbm,
    near_hbm,
    far_hbm,
    hidden_ref,
    attended_ref,
    qkv,
    resid,
    w2,
    wq,
    near,
    far,
    st,
    p1,
    totals,
    p3s,
    p3,
    loc,
    lin2,
    part,
    out_r,
    in_r,
    out_l,
    in_l,
    hg,
    acc,
    sumsq,
    kv,
    kvp,
    load_sem,
    wo_sem,
    wx_send,
    wx_recv,
    s1,
    r1,
    s2,
    r2,
    s3,
    r3,
    lin_send,
    lin_recv,
    rr_send,
    rr_recv,
    rl_send,
    rl_recv,
    gr_send,
    gr_recv,
    gl_send,
    gl_recv,
    gc_send,
    gc_recv,
    kv_send,
    kv_recv,
):
    ny, nx, nz = sizes
    half_z = nz // 2
    y, x, z, c = (lax.axis_index(name) for name in ("y", "x", "z", "c"))
    tok, width = resid.shape
    half = tok // 2
    halves = (pl.ds(0, half), pl.ds(half, half))
    heads = (pl.ds(0, HD), pl.ds(HD, HD))
    other = 1 - c
    right, left = lax.rem(z + 1, nz), lax.rem(z + nz - 1, nz)
    next_x = lax.rem(x + 1, nx)
    next_y = lax.rem(y + (x + 1) // nx, ny)
    prev_x = lax.rem(x + nx - 1, nx)
    prev_y = lax.rem(y + ny - 1 + (x + nx - 1) // nx, ny)
    block = y * nx + x

    load_qkv = pltpu.make_async_copy(qkv_hbm, qkv, load_sem.at[0])
    load_qkv.start()
    barrier = pltpu.get_barrier_semaphore()
    greeted = 0
    places = [{"x": lax.rem(x + k, nx)} for k in range(1, nx)]
    places += [{"y": lax.rem(y + k, ny)} for k in range(1, ny)]
    places += [{"z": right}, {"z": left}, {"c": other}]
    places += [{"y": next_y, "x": next_x}, {"y": prev_y, "x": prev_x}]
    for place in places:
        pl.semaphore_signal(barrier, inc=1, device_id=place, device_id_type=MESH_ID)
        greeted += 1

    load_qkv.wait()
    for h in range(2):
        state = dot(qkv[1, :, heads[h]], qkv[2, :, heads[h]], (0, 0)).astype(BF)
        st[pl.ds(h * nx // 2, nx // 2)] = state.reshape(nx // 2, -1, HD)
    pl.semaphore_wait(barrier, greeted)

    def to_x(k):
        there = lax.rem(x + k, nx)
        return remote(st.at[there], p1.at[x], s1.at[k], r1.at[k], x=there)

    def from_x(k):
        there = lax.rem(x + nx - k, nx)
        return remote(st.at[there], p1.at[there], s1.at[k], r1.at[k], x=there)

    for k in far_first(nx):
        to_x(k).start()
    loads = [
        pltpu.make_async_copy(resid_hbm, resid, load_sem.at[1]),
        pltpu.make_async_copy(near_hbm, near, load_sem.at[2]),
        pltpu.make_async_copy(far_hbm, far, load_sem.at[3]),
        pltpu.make_async_copy(wq_hbm, wq, load_sem.at[4]),
    ]

    def wo_block(j, core):
        return wo_hbm.at[:, pl.ds(pl.multiple_of((2 * j + core) * width, width), width)]

    def wo_own(j):
        return pltpu.make_async_copy(wo_block(j, c), w2.at[j, c], wo_sem.at[j])

    def wo_swap(j, slot):
        return remote(wo_block(j, other), w2.at[j, slot], wx_send.at[j], wx_recv.at[j], c=other)

    for j in range(nz):
        wo_own(j).start()
        wo_swap(j, c).start()
    for load in loads:
        load.start()

    p1[pl.ds(x, 1)] = st[pl.ds(x, 1)]
    rows = lax.broadcasted_iota(jnp.int32, (tok, tok), 0)
    cols = lax.broadcasted_iota(jnp.int32, (tok, tok), 1)
    causal = cols <= rows
    for h in range(2):
        scores = dot(qkv[0, :, heads[h]], qkv[1, :, heads[h]], (1, 1))
        inner = jnp.where(causal, scores, 0.0).astype(BF)
        loc[:, heads[h]] = dot(inner, qkv[2, :, heads[h]])

    for k in far_first(nx)[::-1]:
        from_x(k).wait_recv()
    row_total = p1[0].astype(F32)
    for j in range(1, nx):
        row_total = row_total + p1[j].astype(F32)
    totals[pl.ds(y, 1)] = row_total.astype(BF)[None]

    def to_y(k):
        there = lax.rem(y + k, ny)
        return remote(totals.at[y], totals.at[y], s2.at[k], r2.at[k], y=there)

    def from_y(k):
        there = lax.rem(y + ny - k, ny)
        return remote(totals.at[there], totals.at[there], s2.at[k], r2.at[k], y=there)

    for k in far_first(ny):
        to_y(k).start()

    loads[1].wait()
    loads[2].wait()
    far_cos, far_sin = far[0, pl.ds(block, 1), :], far[1, pl.ds(block, 1), :]
    near_cos, near_sin = near[0], near[1]
    lane = lax.broadcasted_iota(jnp.int32, (tok, HD), 1)
    cosine = far_cos * near_cos - far_sin * near_sin
    sine = far_sin * near_cos + far_cos * near_sin
    near[0] = cosine
    near[1] = jnp.where(lane < HD // 2, -sine, sine)

    for k in far_first(ny)[::-1]:
        from_y(k).wait_recv()
    running = jnp.zeros_like(row_total)
    for j in range(ny):
        running = running + jnp.where(j < y, totals[j].astype(F32), 0.0)
    for j in range(nx):
        p3s[j] = running.astype(BF)
        running = running + p1[j].astype(F32)

    def back_x(k):
        there = lax.rem(x + k, nx)
        return remote(p3s.at[there], p3.at[x], s3.at[k], r3.at[k], x=there)

    def got_x(k):
        there = lax.rem(x + nx - k, nx)
        return remote(p3s.at[there], p3.at[there], s3.at[k], r3.at[k], x=there)

    for k in far_first(nx):
        back_x(k).start()
    p3[pl.ds(x, 1)] = p3s[pl.ds(x, 1)]
    for j in range(nz):
        wo_own(j).wait()
        wo_swap(j, other).wait_recv()
    loads[0].wait()
    for k in far_first(nx)[::-1]:
        got_x(k).wait_recv()

    for h in range(2):
        before = p3[pl.ds(h * nx // 2, nx // 2)].reshape(HD, HD)
        total = loc[:, heads[h]] + dot(qkv[0, :, heads[h]], before)
        lin2[c, :, heads[h]] = (total * scale).astype(BF)

    def lin_swap(slot):
        return remote(lin2.at[c], lin2.at[slot], lin_send, lin_recv, c=other)

    lin_swap(c).start()

    def own_part(j, _):
        part[j] = dot(lin2[c], w2[j, c])
        return 0

    lax.fori_loop(0, nz, own_part, 0)
    lin_swap(other).wait_recv()

    def at(k):
        return lax.rem(z + k + nz, nz)

    def finish_part(k):
        j = at(k)
        part[j] = part[j] + dot(lin2[other], w2[j, other])

    def ring_r(s, h):
        return remote(out_r.at[s, h], in_r.at[s, h], rr_send.at[s, h], rr_recv.at[s, h], z=right)

    def ring_l(s, h):
        return remote(out_l.at[s, h], in_l.at[s, h], rl_send.at[s, h], rl_recv.at[s, h], z=left)

    def pass_r(s, h, first):
        value = part[at(half_z - s), halves[h]]
        if not first:
            ring_r(s - 1, h).wait_recv()
            value = value + in_r[s - 1, h].astype(F32)
        out_r[s, h] = value.astype(BF)
        ring_r(s, h).start()

    def pass_l(s, h, first):
        value = part[at(s - half_z), halves[h]]
        if not first:
            ring_l(s - 1, h).wait_recv()
            value = value + in_l[s - 1, h].astype(F32)
        out_l[s, h] = value.astype(BF)
        ring_l(s, h).start()

    finish_part(half_z)
    pass_r(0, 0, True)
    pass_l(0, 1, True)
    finish_part(half_z - 1)
    pass_r(1, 1, True)
    finish_part(1 - half_z)
    pass_l(1, 0, True)
    for k in range(half_z - 2, 0, -1):
        finish_part(k)
        finish_part(-k)
    finish_part(0)
    pass_r(1, 0, False)
    pass_l(1, 1, False)
    for s in range(2, half_z):
        pass_r(s, 1, False)
        pass_l(s, 0, False)
        pass_r(s, 0, False)
        pass_l(s, 1, False)

    last = half_z - 1
    acc[...] = jnp.zeros_like(acc)
    sumsq[...] = jnp.zeros_like(sumsq)

    def gather_r(s, h):
        return hg.at[at(-s), c, halves[h]]

    def gather_l(s, h):
        return hg.at[at(s), c, halves[h]]

    def send_r(s, h):
        return remote(gather_r(s, h), gather_r(s, h), gr_send.at[s, h], gr_recv.at[s, h], z=right)

    def send_l(s, h):
        return remote(gather_l(s, h), gather_l(s, h), gl_send.at[s, h], gl_recv.at[s, h], z=left)

    def got_r(s, h):
        return remote(gather_r(s + 1, h), gather_r(s + 1, h), gr_send.at[s, h], gr_recv.at[s, h], z=right)

    def got_l(s, h):
        return remote(gather_l(s + 1, h), gather_l(s + 1, h), gl_send.at[s, h], gl_recv.at[s, h], z=left)

    def to_core(k, h):
        piece = hg.at[at(k), c, halves[h]]
        slot = lax.rem(k + nz, nz)
        return remote(piece, piece, gc_send.at[slot, h], gc_recv.at[slot, h], c=other)

    def from_core(k, h):
        piece = hg.at[at(k), other, halves[h]]
        slot = lax.rem(k + nz, nz)
        return remote(piece, piece, gc_send.at[slot, h], gc_recv.at[slot, h], c=other)

    for h in (0, 1):
        if h == 0:
            ring_l(last, 0).wait_recv()
            ring_r(last, 0).wait_recv()
        else:
            ring_r(last, 1).wait_recv()
            ring_l(last, 1).wait_recv()
        mixed = resid[halves[h], :].astype(F32) + part[z, halves[h]]
        mixed = mixed + in_r[last, h].astype(F32) + in_l[last, h].astype(F32)
        mixed = mixed.astype(BF)
        hg[z, c, halves[h]] = mixed
        send_r(0, h).start()
        send_l(0, h).start()
        to_core(0, h).start()
        hidden_ref[halves[h], :] = mixed
    loads[3].wait()

    def project(k, core):
        j = at(k)
        values = hg[j, core]
        rows_of = pl.ds(pl.multiple_of((2 * j + core) * width, width), width)
        for i in range(3):
            acc[i] += dot(values, wq[i, rows_of, :])
        wide = values.astype(F32)
        squares = wide * wide
        sumsq[...] += squares[:, :HD] + squares[:, HD:]

    def project_other(k):
        from_core(k, 0).wait_recv()
        from_core(k, 1).wait_recv()
        project(k, other)

    project(0, c)

    def gather_step(s, _):
        got_r(s, 0).wait_recv()

        @pl.when(s < last)
        def _():
            send_r(s + 1, 0).start()

        got_l(s, 1).wait_recv()

        @pl.when(s < last)
        def _():
            send_l(s + 1, 1).start()

        to_core(-1 - s, 0).start()
        to_core(s + 1, 1).start()

        @pl.when(s < last)
        def _():
            got_r(s, 1).wait_recv()

            @pl.when(s < last - 1)
            def _():
                send_r(s + 1, 1).start()

            got_l(s, 0).wait_recv()

            @pl.when(s < last - 1)
            def _():
                send_l(s + 1, 0).start()

            to_core(-1 - s, 1).start()
            to_core(s + 1, 0).start()

        project(-1 - s, c)

        @pl.when(s < last)
        def _():
            project(s + 1, c)

        @pl.when(s == 0)
        def _():
            project_other(0)

        @pl.when(s > 0)
        def _():
            project_other(-s)
            project_other(s)

        return 0

    lax.fori_loop(0, half_z, gather_step, 0)
    project_other(half_z)

    mean = jnp.sum(sumsq[...], axis=1, keepdims=True) / (width * 2 * nz)
    row_scale = lax.rsqrt(mean + 1e-05)

    def rotated(i, h):
        values = acc[i, :, heads[h]] * row_scale
        return (values * near[0] + pltpu.roll(values, HD // 2, 1) * near[1]).astype(BF)

    def kv_copy(i):
        return remote(kv.at[i], kvp.at[i], kv_send.at[i], kv_recv.at[i], y=next_y, x=next_x)

    for h in range(2):
        kv[0, :, heads[h]] = rotated(1, h)
    kv_copy(0).start()
    kv[1] = (acc[2] * row_scale).astype(BF)
    kv_copy(1).start()

    score_scale = 1.0 / math.sqrt(HD)
    queries, tops, sums, outs = [], [], [], []
    for h in range(2):
        q = rotated(0, h)
        logits = jnp.where(causal, dot(q, kv[0, :, heads[h]], (1, 1)) * score_scale, -1e30)
        top = jnp.max(logits, axis=1, keepdims=True)
        expo = jnp.exp(logits - top)
        queries.append(q)
        tops.append(top)
        sums.append(jnp.sum(expo, axis=1, keepdims=True))
        outs.append(dot(expo.astype(BF), kv[1, :, heads[h]]))
    kv_copy(0).wait_recv()
    weights = []
    for h in range(2):
        logits = dot(queries[h], kvp[0, :, heads[h]], (1, 1)) * score_scale
        logits = jnp.where(block > 0, logits, -1e30)
        top = jnp.maximum(tops[h], jnp.max(logits, axis=1, keepdims=True))
        expo = jnp.exp(logits - top)
        old = jnp.exp(tops[h] - top)
        sums[h] = sums[h] * old + jnp.sum(expo, axis=1, keepdims=True)
        outs[h] = outs[h] * old
        weights.append(expo.astype(BF))
    kv_copy(1).wait_recv()
    for h in range(2):
        out = outs[h] + dot(weights[h], kvp[1, :, heads[h]])
        attended_ref[:, heads[h]] = (out / sums[h]).astype(BF)

    for k in range(1, nx):
        to_x(k).wait_send()
        back_x(k).wait_send()
    for k in range(1, ny):
        to_y(k).wait_send()
    for j in range(nz):
        wo_swap(j, c).wait_send()
    lin_swap(c).wait_send()
    for s in range(half_z):
        for h in range(2):
            if s or h == 0:
                ring_r(s, h).wait_send()
            if s or h == 1:
                ring_l(s, h).wait_send()
            if s < last or h == 0:
                send_r(s, h).wait_send()
            if s < last or h == 1:
                send_l(s, h).wait_send()
    for k in range(nz):
        for h in range(2):
            to_core(k, h).wait_send()
    for i in range(2):
        kv_copy(i).wait_send()


def tables(tok, blocks):
    freq = 500000.0 ** (-(np.arange(HD // 2) * 2.0 / HD))
    freq = np.concatenate([freq, freq])
    near = np.arange(tok)[:, None] * freq
    far = (np.arange(blocks) * tok)[:, None] * freq
    return tuple(np.stack([np.cos(a), np.sin(a)]).astype(np.float32) for a in (near, far))


def local(sizes, lin_qkv, resid, w_out, w_qkv):
    ny, nx, nz = sizes
    tok, width = resid.shape
    half_z = nz // 2
    near, far = tables(tok, ny * nx)
    scale = 1.0 / math.sqrt(HD * tok * ny * nx)
    rows = 2 * HD // nx
    anywhere = pl.BlockSpec(memory_space=pl.ANY)
    dma = pltpu.SemaphoreType.DMA
    vmem = pltpu.VMEM
    scratch = [
        vmem((3, tok, width), BF),
        vmem((tok, width), BF),
        vmem((nz, 2, width, width), BF),
        vmem((3, 2 * nz * width, width), BF),
        vmem(near.shape, F32),
        vmem(far.shape, F32),
        vmem((nx, rows, HD), BF),
        vmem((nx, rows, HD), BF),
        vmem((ny, rows, HD), BF),
        vmem((nx, rows, HD), BF),
        vmem((nx, rows, HD), BF),
        vmem((tok, width), F32),
        vmem((2, tok, width), BF),
        vmem((nz, tok, width), F32),
        vmem((half_z, 2, tok // 2, width), BF),
        vmem((half_z, 2, tok // 2, width), BF),
        vmem((half_z, 2, tok // 2, width), BF),
        vmem((half_z, 2, tok // 2, width), BF),
        vmem((nz, 2, tok, width), BF),
        vmem((3, tok, width), F32),
        vmem((tok, HD), F32),
        vmem((2, tok, width), BF),
        vmem((2, tok, width), BF),
        dma((5,)),
        dma((nz,)),
        dma((nz,)),
        dma((nz,)),
        dma((nx,)),
        dma((nx,)),
        dma((ny,)),
        dma((ny,)),
        dma((nx,)),
        dma((nx,)),
        dma,
        dma,
        dma((half_z, 2)),
        dma((half_z, 2)),
        dma((half_z, 2)),
        dma((half_z, 2)),
        dma((half_z, 2)),
        dma((half_z, 2)),
        dma((half_z, 2)),
        dma((half_z, 2)),
        dma((nz, 2)),
        dma((nz, 2)),
        dma((2,)),
        dma((2,)),
    ]
    return pl.pallas_call(
        functools.partial(layer_pair, sizes, scale),
        name="layer_pair",
        out_shape=(jax.ShapeDtypeStruct((tok, width), BF),) * 2,
        in_specs=[anywhere] * 6,
        out_specs=(pl.BlockSpec(memory_space=pltpu.VMEM),) * 2,
        scratch_shapes=scratch,
        compiler_params=pltpu.CompilerParams(
            collective_id=0, has_side_effects=True, vmem_limit_bytes=48 * 1024 * 1024
        ),
    )(
        jnp.transpose(lin_qkv, (1, 0, 2)),
        resid,
        w_out,
        jnp.transpose(w_qkv, (1, 0, 2)),
        jnp.asarray(near),
        jnp.asarray(far),
    )


def on_torus(devices, sizes):
    finer = Mesh(devices.reshape(*sizes, 2), ("y", "x", "z", "c"))
    seq, head = ("y", "x"), ("z", "c")
    return jax.shard_map(
        functools.partial(local, sizes),
        mesh=finer,
        in_specs=(P(seq, None, head), P(seq, head), P(head, None), P(None, None, head)),
        out_specs=(P(seq, head), P(seq, head)),
        check_vma=False,
    )


def solution(mesh):
    side = math.isqrt(mesh.shape["seq"])
    return on_torus(mesh.devices, (side, side, mesh.shape["head"] // 2))
```

time: 250 us -> 89.2 us (0.36); the launches traced: 246 us -> 88.9 us
  waiting for transfers between devices: 109 us -> 0 us
  Pallas kernels: 0 us -> 81.6 us
  blocking collectives: 64.6 us -> 0 us
  starting transfers between devices: 24.5 us -> 0 us
  between operations: 14 us -> 0.65 us
  local copies, waits for them, and re-layouts: 17.7 us -> 6.58 us
  matrix products: 10.4 us -> 0 us
  other arithmetic: 5.13 us -> 0 us
    all_gather x3 -> x0, waiting for transfers between devices: 108 us -> none  [the longest x2 73.4 us: entering(): pieces = lax.all_gather(so_far, axis)]
    pallas_call x0 -> x1, Pallas kernels: none -> 81.6 us  [local(): pl.pallas_call(functools.partial(layer_pair, sizes, scale), name='layer_p...]
    all_to_all x1 -> x0, blocking collectives: 64.6 us -> none  [from_everyone(): lax.all_to_all(jnp.broadcast_to(array[None], (devices, *array.shape)), ax...]
    all_to_all x1 -> x0, starting transfers between devices: 18.2 us -> none  [local(): lax.all_to_all(w_out, 'head', split_axis=1, concat_axis=0, tiled=True)]
    dot_general x6 -> x0, matrix products: 9.66 us -> none  [the longest x1 4.68 us: local(): proj = jnp.dot(normed, flat_w, preferred_element_type=jnp.float32)]
    unnamed x9 -> x12, local copies, waits for them, and re-layouts: 13.7 us -> 6.58 us
    ppermute x2 -> x0, starting transfers between devices: 6.19 us -> none  [shifted(): return lax.ppermute(array, axis, pairs)]
    reduce_sum x1 -> x0, other arithmetic: 2.7 us -> none  [local(): meansq = jnp.sum(whole * whole, axis=1, keepdims=True) / D]
  transfers between devices with their start and end apart: 6 -> 0, of which waited for: 4 -> 0; matrix products, arithmetic and copies ran while one was open for 8% -> 0% of each run, Pallas kernels for 0% -> 0%
where the time goes in v1:
time: 89.2 us; the launch traced here: 88.9 us
  Pallas kernels  81.6 us (91%)
  local copies, waits for them, and re-layouts  6.58 us (7%)
    pallas_call x1, Pallas kernels, local(): pl.pallas_call(functools.partial(layer_pair, sizes, scale), name='layer_p...  81.6 us
    unnamed x12, local copies, waits for them, and re-layouts  6.58 us

profile of v1, /device:TPU:1, one launch (start us, length us, event | category | flops | bytes accessed | tf_op | source)
XLA Modules:
  0.0 88.9 jit_solution(12823350828766112150)
XLA Ops:
  0.6 0.0 copy-start
  0.6 1.6 %copy-done = bf16[256,4096]{1,0:T(8,128)(2,1)S(1)} copy-done((bf16[256,4096]{1,0:T(8,128)(2,1)S(1)}, bf16[256,4096]{1,0:T(8,128)(2,1)}, u32[]{:S(2)}) %copy-start) | copy-done | bytes 2097176
  2.2 0.0 copy-start.1
  2.2 1.0 %copy-done.1 = bf16[256,3,256]{2,0,1:T(8,128)(2,1)S(1)} copy-done((bf16[256,3,256]{2,0,1:T(8,128)(2,1)S(1)}, bf16[256,3,256]{2,0,1:T(8,128)(2,1)}, u32[]{:S(2)}) %copy-start.1) | copy-done | bytes 393240
  3.2 0.0 copy-start.2
  3.2 0.9 %copy-done.2 = f32[2,256,128]{2,1,0:T(8,128)S(1)} copy-done((f32[2,256,128]{2,1,0:T(8,128)S(1)}, f32[2,256,128]{2,1,0:T(8,128)}, u32[]{:S(2)}) %copy-start.2) | copy-done | bytes 262168
  4.2 0.0 copy-start.3
  4.2 0.9 %copy-done.3 = bf16[256,256]{1,0:T(8,128)(2,1)S(1)} copy-done((bf16[256,256]{1,0:T(8,128)(2,1)S(1)}, bf16[256,256]{1,0:T(8,128)(2,1)}, u32[]{:S(2)}) %copy-start.3) | copy-done | bytes 131096
  5.1 0.0 copy-start.4
  5.1 0.8 copy-done.4
  5.9 81.6 %layer_pair.1 = (bf16[256,256]{1,0:T(8,128)(2,1)S(1)}, bf16[256,256]{1,0:T(8,128)(2,1)S(1)}) custom-call(bf16[3,256,256]{2,1,0:T(8,128)(2,1)S(1)} %bitcast.2, bf16[256,256]{1,0:T(8,128)(2,1)S(1)} %copy-done.3, bf16[256,4096]{1,0:T(8,128)(2,1)S(1)} %copy-done, bf16[3,4096,256]{2,1,0:T(8,128)(2,1)} %bitcast.3, f32[2,256,128]{2,1,0:T(8,128)S(1)} %copy-done.2, ...), custom_call_target="tpu_custom_call" | custom-call | tf_op jit(solution)/shard_map/layer_pair/pallas_call | solution.py:541
  87.6 0.7 copy.10
  88.2 0.7 copy.11
Async XLA Ops:
  0.6 1.6 %copy-start = (bf16[256,4096]{1,0:T(8,128)(2,1)S(1)}, bf16[256,4096]{1,0:T(8,128)(2,1)}, u32[]{:S(2)}) copy-start(bf16[256,4096]{1,0:T(8,128)(2,1)} %wo_hbm.1) | copy-start | bytes 6291460
  2.2 1.0 %copy-start.1 = (bf16[256,3,256]{2,0,1:T(8,128)(2,1)S(1)}, bf16[256,3,256]{2,0,1:T(8,128)(2,1)}, u32[]{:S(2)}) copy-start(bf16[256,3,256]{2,0,1:T(8,128)(2,1)} %param.6) | copy-start | bytes 1179652
  3.2 0.9 %copy-start.2 = (f32[2,256,128]{2,1,0:T(8,128)S(1)}, f32[2,256,128]{2,1,0:T(8,128)}, u32[]{:S(2)}) copy-start(f32[2,256,128]{2,1,0:T(8,128)} %constant.4.clone.near_hbm) | copy-start | bytes 786436
  4.2 0.9 %copy-start.3 = (bf16[256,256]{1,0:T(8,128)(2,1)S(1)}, bf16[256,256]{1,0:T(8,128)(2,1)}, u32[]{:S(2)}) copy-start(bf16[256,256]{1,0:T(8,128)(2,1)} %resid_hbm.1) | copy-start | bytes 393220
  5.1 0.8 copy-start.4

commit v2 on v1

v2 whole, which is shorter than its diff:
```python
import functools
import math

import jax
import jax.numpy as jnp
import numpy as np
from jax import lax
from jax.experimental import pallas as pl
from jax.experimental.pallas import tpu as pltpu
from jax.sharding import Mesh
from jax.sharding import PartitionSpec as P

HD = 128
BF = jnp.bfloat16
F32 = jnp.float32
MESH_ID = pl.DeviceIdType.MESH
PIECES = 4


def dot(a, b, contract=(1, 0)):
    dims = (((contract[0],), (contract[1],)), ((), ()))
    return lax.dot_general(a, b, dims, preferred_element_type=F32)


def remote(src, dst, send, recv, **where):
    return pltpu.make_async_remote_copy(
        src_ref=src, dst_ref=dst, send_sem=send, recv_sem=recv, device_id=where, device_id_type=MESH_ID
    )


def far_first(n):
    return sorted(range(1, n), key=lambda k: -min(k, n - k))


def layer_pair(
    sizes,
    scale,
    qkv_hbm,
    resid_hbm,
    wo_hbm,
    wq_hbm,
    near_hbm,
    far_hbm,
    hidden_ref,
    attended_ref,
    qkv,
    resid,
    w2,
    wq,
    near,
    far,
    st,
    p1,
    totals,
    p3s,
    p3,
    loc,
    lin2,
    part,
    out_r,
    in_r,
    out_l,
    in_l,
    hg,
    acc,
    sumsq,
    kv,
    kvp,
    qr,
    load_sem,
    wo_sem,
    wx_send,
    wx_recv,
    s1,
    r1,
    s2,
    r2,
    s3,
    r3,
    lin_send,
    lin_recv,
    rr_send,
    rr_recv,
    rl_send,
    rl_recv,
    gr_send,
    gr_recv,
    gl_send,
    gl_recv,
    gc_send,
    gc_recv,
    kv_send,
    kv_recv,
):
    ny, nx, nz = sizes
    half_z = nz // 2
    y, x, z, c = (lax.axis_index(name) for name in ("y", "x", "z", "c"))
    tok, width = resid.shape
    half = tok // 2
    halves = (pl.ds(0, half), pl.ds(half, half))
    rows_in = tok // PIECES
    piece_rows = [pl.ds(p * rows_in, rows_in) for p in range(PIECES)]
    early, late = list(range(PIECES // 2)), list(range(PIECES // 2, PIECES))
    heads = (pl.ds(0, HD), pl.ds(HD, HD))
    other = 1 - c
    right, left = lax.rem(z + 1, nz), lax.rem(z + nz - 1, nz)
    next_x = lax.rem(x + 1, nx)
    next_y = lax.rem(y + (x + 1) // nx, ny)
    prev_x = lax.rem(x + nx - 1, nx)
    prev_y = lax.rem(y + ny - 1 + (x + nx - 1) // nx, ny)
    block = y * nx + x

    sent = []

    def go(copy):
        copy.start()
        sent.append(copy)

    load_qkv = pltpu.make_async_copy(qkv_hbm, qkv, load_sem.at[0])
    load_qkv.start()
    barrier = pltpu.get_barrier_semaphore()
    greeted = 0
    places = [{"x": lax.rem(x + k, nx)} for k in range(1, nx)]
    places += [{"y": lax.rem(y + k, ny)} for k in range(1, ny)]
    places += [{"z": right}, {"z": left}, {"c": other}]
    places += [{"y": next_y, "x": next_x}, {"y": prev_y, "x": prev_x}]
    for place in places:
        pl.semaphore_signal(barrier, inc=1, device_id=place, device_id_type=MESH_ID)
        greeted += 1

    load_qkv.wait()
    for h in range(2):
        state = dot(qkv[1, :, heads[h]], qkv[2, :, heads[h]], (0, 0)).astype(BF)
        st[pl.ds(h * nx // 2, nx // 2)] = state.reshape(nx // 2, -1, HD)
    pl.semaphore_wait(barrier, greeted)

    def to_x(k):
        there = lax.rem(x + k, nx)
        return remote(st.at[there], p1.at[x], s1.at[k], r1.at[k], x=there)

    def from_x(k):
        there = lax.rem(x + nx - k, nx)
        return remote(st.at[there], p1.at[there], s1.at[k], r1.at[k], x=there)

    for k in far_first(nx):
        go(to_x(k))
    loads = [
        pltpu.make_async_copy(resid_hbm, resid, load_sem.at[1]),
        pltpu.make_async_copy(near_hbm, near, load_sem.at[2]),
        pltpu.make_async_copy(far_hbm, far, load_sem.at[3]),
        pltpu.make_async_copy(wq_hbm, wq, load_sem.at[4]),
    ]

    def wo_block(j, core):
        return wo_hbm.at[:, pl.ds(pl.multiple_of((2 * j + core) * width, width), width)]

    def wo_own(j):
        return pltpu.make_async_copy(wo_block(j, c), w2.at[j, c], wo_sem.at[j])

    def wo_swap(j, slot):
        return remote(wo_block(j, other), w2.at[j, slot], wx_send.at[j], wx_recv.at[j], c=other)

    for j in range(nz):
        wo_own(j).start()
        go(wo_swap(j, c))
    for load in loads:
        load.start()

    p1[pl.ds(x, 1)] = st[pl.ds(x, 1)]
    rows = lax.broadcasted_iota(jnp.int32, (tok, tok), 0)
    cols = lax.broadcasted_iota(jnp.int32, (tok, tok), 1)
    causal = cols <= rows
    for h in range(2):
        scores = dot(qkv[0, :, heads[h]], qkv[1, :, heads[h]], (1, 1))
        inner = jnp.where(causal, scores, 0.0).astype(BF)
        loc[:, heads[h]] = dot(inner, qkv[2, :, heads[h]])

    for k in far_first(nx)[::-1]:
        from_x(k).wait_recv()
    row_total = p1[0].astype(F32)
    for j in range(1, nx):
        row_total = row_total + p1[j].astype(F32)
    totals[pl.ds(y, 1)] = row_total.astype(BF)[None]

    def to_y(k):
        there = lax.rem(y + k, ny)
        return remote(totals.at[y], totals.at[y], s2.at[k], r2.at[k], y=there)

    def from_y(k):
        there = lax.rem(y + ny - k, ny)
        return remote(totals.at[there], totals.at[there], s2.at[k], r2.at[k], y=there)

    for k in far_first(ny):
        go(to_y(k))

    loads[1].wait()
    loads[2].wait()
    far_cos, far_sin = far[0, pl.ds(block, 1), :], far[1, pl.ds(block, 1), :]
    near_cos, near_sin = near[0], near[1]
    lane = lax.broadcasted_iota(jnp.int32, (tok, HD), 1)
    cosine = far_cos * near_cos - far_sin * near_sin
    sine = far_sin * near_cos + far_cos * near_sin
    near[0] = cosine
    near[1] = jnp.where(lane < HD // 2, -sine, sine)

    for k in far_first(ny)[::-1]:
        from_y(k).wait_recv()
    running = jnp.zeros_like(row_total)
    for j in range(ny):
        running = running + jnp.where(j < y, totals[j].astype(F32), 0.0)
    for j in range(nx):
        p3s[j] = running.astype(BF)
        running = running + p1[j].astype(F32)

    def back_x(k):
        there = lax.rem(x + k, nx)
        return remote(p3s.at[there], p3.at[x], s3.at[k], r3.at[k], x=there)

    def got_x(k):
        there = lax.rem(x + nx - k, nx)
        return remote(p3s.at[there], p3.at[there], s3.at[k], r3.at[k], x=there)

    for k in far_first(nx):
        go(back_x(k))
    p3[pl.ds(x, 1)] = p3s[pl.ds(x, 1)]
    for j in range(nz):
        wo_own(j).wait()
        wo_swap(j, other).wait_recv()
    loads[0].wait()
    for k in far_first(nx)[::-1]:
        got_x(k).wait_recv()

    for h in range(2):
        before = p3[pl.ds(h * nx // 2, nx // 2)].reshape(HD, HD)
        total = loc[:, heads[h]] + dot(qkv[0, :, heads[h]], before)
        lin2[c, :, heads[h]] = (total * scale).astype(BF)

    def lin_swap(slot):
        return remote(lin2.at[c], lin2.at[slot], lin_send, lin_recv, c=other)

    go(lin_swap(c))

    def own_part(j, _):
        part[j] = dot(lin2[c], w2[j, c])
        return 0

    lax.fori_loop(0, nz, own_part, 0)
    lin_swap(other).wait_recv()

    def at(k):
        return lax.rem(z + k + nz, nz)

    def finish_part(k):
        j = at(k)
        part[j] = part[j] + dot(lin2[other], w2[j, other])

    def ring_r(s, p):
        return remote(out_r.at[s, p], in_r.at[s, p], rr_send.at[s, p], rr_recv.at[s, p], z=right)

    def ring_l(s, p):
        return remote(out_l.at[s, p], in_l.at[s, p], rl_send.at[s, p], rl_recv.at[s, p], z=left)

    def pass_r(s, p, first=False):
        value = part[at(half_z - s), piece_rows[p]]
        if not first:
            ring_r(s - 1, p).wait_recv()
            value = value + in_r[s - 1, p].astype(F32)
        out_r[s, p] = value.astype(BF)
        go(ring_r(s, p))

    def pass_l(s, p, first=False):
        value = part[at(s - half_z), piece_rows[p]]
        if not first:
            ring_l(s - 1, p).wait_recv()
            value = value + in_l[s - 1, p].astype(F32)
        out_l[s, p] = value.astype(BF)
        go(ring_l(s, p))

    finish_part(half_z)
    for p, q in zip(early, late):
        pass_r(0, p, True)
        pass_l(0, q, True)
    finish_part(half_z - 1)
    for q in late:
        pass_r(1, q, True)
    finish_part(1 - half_z)
    for p in early:
        pass_l(1, p, True)
    for k in range(half_z - 2, 0, -1):
        finish_part(k)
        finish_part(-k)
    finish_part(0)
    for p, q in zip(early, late):
        pass_r(1, p)
        pass_l(1, q)
    for s in range(2, half_z):
        for p, q in zip(early, late):
            pass_r(s, q)
            pass_l(s, p)
        for p, q in zip(early, late):
            pass_r(s, p)
            pass_l(s, q)

    last = half_z - 1
    acc[...] = jnp.zeros_like(acc)
    sumsq[...] = jnp.zeros_like(sumsq)

    def piece(k, core, p):
        return hg.at[at(k), core, piece_rows[p]]

    def send_r(s, p):
        return remote(piece(-s, c, p), piece(-s, c, p), gr_send.at[s, p], gr_recv.at[s, p], z=right)

    def send_l(s, p):
        return remote(piece(s, c, p), piece(s, c, p), gl_send.at[s, p], gl_recv.at[s, p], z=left)

    def got_r(s, p):
        here = piece(-s - 1, c, p)
        remote(here, here, gr_send.at[s, p], gr_recv.at[s, p], z=right).wait_recv()

    def got_l(s, p):
        here = piece(s + 1, c, p)
        remote(here, here, gl_send.at[s, p], gl_recv.at[s, p], z=left).wait_recv()

    def core_copy(k, core, p):
        slot = lax.rem(k + nz, nz)
        here = piece(k, core, p)
        return remote(here, here, gc_send.at[slot, p], gc_recv.at[slot, p], c=other)

    for p in range(PIECES):
        if p in early:
            ring_l(last, p).wait_recv()
            ring_r(last, p).wait_recv()
        else:
            ring_r(last, p).wait_recv()
            ring_l(last, p).wait_recv()
        mixed = resid[piece_rows[p], :].astype(F32) + part[z, piece_rows[p]]
        mixed = mixed + in_r[last, p].astype(F32) + in_l[last, p].astype(F32)
        mixed = mixed.astype(BF)
        hg[z, c, piece_rows[p]] = mixed
        go(send_r(0, p))
        go(send_l(0, p))
        go(core_copy(0, c, p))
        hidden_ref[piece_rows[p], :] = mixed
    loads[3].wait()

    def project(k, core, h):
        j = at(k)
        values = hg[j, core, halves[h]]
        rows_of = pl.ds(pl.multiple_of((2 * j + core) * width, width), width)
        for i in range(3):
            acc[i, halves[h]] += dot(values, wq[i, rows_of, :])
        wide = values.astype(F32)
        squares = wide * wide
        sumsq[halves[h]] += squares[:, :HD] + squares[:, HD:]

    def project_other(k, h):
        for p in (early, late)[h]:
            core_copy(k, other, p).wait_recv()
        project(k, other, h)

    project(0, c, 0)
    project(0, c, 1)

    def gather_step(s, _):
        for h in range(2):
            for p in (early, late)[h]:
                got_r(s, p)
                if h == 0:
                    send_r(s + 1, p).start()
                else:
                    pl.when(s < last - 1)(lambda p=p: send_r(s + 1, p).start())
                core_copy(-1 - s, c, p).start()
                got_l(s, p)
                if h == 1:
                    send_l(s + 1, p).start()
                else:
                    pl.when(s < last - 1)(lambda p=p: send_l(s + 1, p).start())
                core_copy(s + 1, c, p).start()
            project(-1 - s, c, h)
            project(s + 1, c, h)
            project_other(-s, h)
            pl.when(s > 0)(lambda h=h: project_other(s, h))
        return 0

    lax.fori_loop(0, last, gather_step, 0)
    for s in range(1, half_z):
        sent += [send_r(s, p) for p in early]
        sent += [send_l(s, q) for q in late]
        if s < last:
            sent += [send_r(s, q) for q in late]
            sent += [send_l(s, p) for p in early]
    for k in range(1, nz):
        sent += [core_copy(k, c, p) for p in range(PIECES) if k != half_z]

    def kv_copy(h, i):
        return remote(kv.at[h, i], kvp.at[h, i], kv_send.at[h, i], kv_recv.at[h, i], y=next_y, x=next_x)

    def row_scale(h):
        mean = jnp.sum(sumsq[halves[h]], axis=1, keepdims=True) / (width * 2 * nz)
        return lax.rsqrt(mean + 1e-05)

    def rotated(i, h, head, scaled):
        values = acc[i, halves[h], heads[head]] * scaled
        return (values * near[0, halves[h]] + pltpu.roll(values, HD // 2, 1) * near[1, halves[h]]).astype(BF)

    for h in range(2):
        for p in (early, late)[h]:
            if h == 0:
                got_r(last, p)
            else:
                got_l(last, p)
            go(core_copy(half_z, c, p))
        project(half_z, c, h)
        project_other(-last, h)
        project_other(last, h)
        project_other(half_z, h)
        scaled = row_scale(h)
        for head in range(2):
            kv[h, 0, :, heads[head]] = rotated(1, h, head, scaled)
        go(kv_copy(h, 0))
        kv[h, 1] = (acc[2, halves[h]] * scaled).astype(BF)
        go(kv_copy(h, 1))
        for head in range(2):
            qr[halves[h], heads[head]] = rotated(0, h, head, scaled)

    score_scale = 1.0 / math.sqrt(HD)
    tops, sums, outs = [], [], []
    for head in range(2):
        q = qr[:, heads[head]]
        logits = []
        for h in range(2):
            value = dot(q, kv[h, 0, :, heads[head]], (1, 1)) * score_scale
            logits.append(jnp.where(causal[:, h * half : (h + 1) * half], value, -1e30))
        top = jnp.maximum(*(jnp.max(value, axis=1, keepdims=True) for value in logits))
        expos = [jnp.exp(value - top) for value in logits]
        tops.append(top)
        sums.append(sum(jnp.sum(expo, axis=1, keepdims=True) for expo in expos))
        outs.append(sum(dot(expos[h].astype(BF), kv[h, 1, :, heads[head]]) for h in range(2)))
    for h in range(2):
        kv_copy(h, 0).wait_recv()
        weights = []
        for head in range(2):
            logits = dot(qr[:, heads[head]], kvp[h, 0, :, heads[head]], (1, 1)) * score_scale
            logits = jnp.where(block > 0, logits, -1e30)
            top = jnp.maximum(tops[head], jnp.max(logits, axis=1, keepdims=True))
            expo = jnp.exp(logits - top)
            old = jnp.exp(tops[head] - top)
            tops[head] = top
            sums[head] = sums[head] * old + jnp.sum(expo, axis=1, keepdims=True)
            outs[head] = outs[head] * old
            weights.append(expo.astype(BF))
        kv_copy(h, 1).wait_recv()
        for head in range(2):
            outs[head] = outs[head] + dot(weights[head], kvp[h, 1, :, heads[head]])
    for head in range(2):
        attended_ref[:, heads[head]] = (outs[head] / sums[head]).astype(BF)

    for copy in sent:
        copy.wait_send()


def tables(tok, blocks):
    freq = 500000.0 ** (-(np.arange(HD // 2) * 2.0 / HD))
    freq = np.concatenate([freq, freq])
    near = np.arange(tok)[:, None] * freq
    far = (np.arange(blocks) * tok)[:, None] * freq
    return tuple(np.stack([np.cos(a), np.sin(a)]).astype(np.float32) for a in (near, far))


def local(sizes, lin_qkv, resid, w_out, w_qkv):
    ny, nx, nz = sizes
    tok, width = resid.shape
    half_z = nz // 2
    near, far = tables(tok, ny * nx)
    scale = 1.0 / math.sqrt(HD * tok * ny * nx)
    rows = 2 * HD // nx
    anywhere = pl.BlockSpec(memory_space=pltpu.HBM)
    dma = pltpu.SemaphoreType.DMA
    vmem = pltpu.VMEM
    scratch = [
        vmem((3, tok, width), BF),
        vmem((tok, width), BF),
        vmem((nz, 2, width, width), BF),
        vmem((3, 2 * nz * width, width), BF),
        vmem(near.shape, F32),
        vmem(far.shape, F32),
        vmem((nx, rows, HD), BF),
        vmem((nx, rows, HD), BF),
        vmem((ny, rows, HD), BF),
        vmem((nx, rows, HD), BF),
        vmem((nx, rows, HD), BF),
        vmem((tok, width), F32),
        vmem((2, tok, width), BF),
        vmem((nz, tok, width), F32),
        vmem((half_z, PIECES, tok // PIECES, width), BF),
        vmem((half_z, PIECES, tok // PIECES, width), BF),
        vmem((half_z, PIECES, tok // PIECES, width), BF),
        vmem((half_z, PIECES, tok // PIECES, width), BF),
        vmem((nz, 2, tok, width), BF),
        vmem((3, tok, width), F32),
        vmem((tok, HD), F32),
        vmem((2, 2, tok // 2, width), BF),
        vmem((2, 2, tok // 2, width), BF),
        vmem((tok, width), BF),
        dma((5,)),
        dma((nz,)),
        dma((nz,)),
        dma((nz,)),
        dma((nx,)),
        dma((nx,)),
        dma((ny,)),
        dma((ny,)),
        dma((nx,)),
        dma((nx,)),
        dma,
        dma,
        dma((half_z, PIECES)),
        dma((half_z, PIECES)),
        dma((half_z, PIECES)),
        dma((half_z, PIECES)),
        dma((half_z, PIECES)),
        dma((half_z, PIECES)),
        dma((half_z, PIECES)),
        dma((half_z, PIECES)),
        dma((nz, PIECES)),
        dma((nz, PIECES)),
        dma((2, 2)),
        dma((2, 2)),
    ]
    operands = (
        jnp.transpose(lin_qkv, (1, 0, 2)),
        resid,
        w_out,
        jnp.transpose(w_qkv, (1, 0, 2)),
        jnp.asarray(near),
        jnp.asarray(far),
    )
    return pl.pallas_call(
        functools.partial(layer_pair, sizes, scale),
        name="layer_pair",
        out_shape=(jax.ShapeDtypeStruct((tok, width), BF),) * 2,
        in_specs=[anywhere] * 6,
        out_specs=(pl.BlockSpec(memory_space=pltpu.VMEM),) * 2,
        scratch_shapes=scratch,
        compiler_params=pltpu.CompilerParams(
            collective_id=0, has_side_effects=True, vmem_limit_bytes=48 * 1024 * 1024
        ),
    )(
        *(pltpu.with_memory_space_constraint(array, pltpu.HBM) for array in operands)
    )


def on_torus(devices, sizes):
    finer = Mesh(devices.reshape(*sizes, 2), ("y", "x", "z", "c"))
    seq, head = ("y", "x"), ("z", "c")
    return jax.shard_map(
        functools.partial(local, sizes),
        mesh=finer,
        in_specs=(P(seq, None, head), P(seq, head), P(head, None), P(None, None, head)),
        out_specs=(P(seq, head), P(seq, head)),
        check_vma=False,
    )


def solution(mesh):
    side = math.isqrt(mesh.shape["seq"])
    return on_torus(mesh.devices, (side, side, mesh.shape["head"] // 2))
```

time: 89.2 us -> 81.8 us (0.917)
  local copies, waits for them, and re-layouts: 6.58 us -> 1.31 us
  Pallas kernels: 81.6 us -> 79.6 us
    unnamed x12 -> x2, local copies, waits for them, and re-layouts: 6.58 us -> 1.31 us
    pallas_call x1, Pallas kernels: 81.6 us -> 79.6 us  [local(): pl.pallas_call(functools.partial(layer_pair, sizes, scale), name='layer_p...]
where the time goes in v2:
time: 81.8 us; the launch traced here: 81.6 us
  Pallas kernels  79.6 us (97%)
  local copies, waits for them, and re-layouts  1.31 us (2%)
    pallas_call x1, Pallas kernels, local(): pl.pallas_call(functools.partial(layer_pair, sizes, scale), name='layer_p...  79.6 us

profile of v2, /device:TPU:1, one launch (start us, length us, event | category | flops | bytes accessed | tf_op | source)
XLA Modules:
  0.0 81.6 jit_solution(7721711085953225705)
XLA Ops:
  0.6 79.6 %layer_pair.1 = (bf16[256,256]{1,0:T(8,128)(2,1)S(1)}, bf16[256,256]{1,0:T(8,128)(2,1)S(1)}) custom-call(bf16[3,256,256]{2,1,0:T(8,128)(2,1)} %bitcast.3, bf16[256,256]{1,0:T(8,128)(2,1)} %resid_hbm.1, bf16[256,4096]{1,0:T(8,128)(2,1)} %wo_hbm.1, bf16[3,4096,256]{2,1,0:T(8,128)(2,1)} %bitcast.2, f32[2,256,128]{2,1,0:T(8,128)} %constant.4.clone.near_hbm, ...), custom_call_target="tpu_custom_call" | custom-call | tf_op jit(solution)/shard_map/layer_pair/pallas_call | solution.py:539
  80.3 0.7 copy.10
  80.9 0.7 copy.11

commit v3 on v2

--- a/solution.py
+++ b/solution.py
@@ -61,6 +61,8 @@
     in_r,
     out_l,
     in_l,
+    far_out,
+    far_in,
     hg,
     acc,
     sumsq,
@@ -83,6 +85,8 @@
     rr_recv,
     rl_send,
     rl_recv,
+    rf_send,
+    rf_recv,
     gr_send,
     gr_recv,
     gl_send,
@@ -122,7 +126,7 @@
     greeted = 0
     places = [{"x": lax.rem(x + k, nx)} for k in range(1, nx)]
     places += [{"y": lax.rem(y + k, ny)} for k in range(1, ny)]
-    places += [{"z": right}, {"z": left}, {"c": other}]
+    places += [{"z": right}, {"z": left}, {"z": lax.rem(z + 2, nz)}, {"z": lax.rem(z + nz - 2, nz)}, {"c": other}]
     places += [{"y": next_y, "x": next_x}, {"y": prev_y, "x": prev_x}]
     for place in places:
         pl.semaphore_signal(barrier, inc=1, device_id=place, device_id_type=MESH_ID)
@@ -190,8 +194,8 @@
         there = lax.rem(y + ny - k, ny)
         return remote(totals.at[there], totals.at[there], s2.at[k], r2.at[k], y=there)
 
-    for k in far_first(ny):
-        go(to_y(k))
+    for k in range(ny - 1, 0, -1):
+        pl.when(y < ny - k)(lambda k=k: to_y(k).start())
 
     loads[1].wait()
     loads[2].wait()
@@ -203,8 +207,8 @@
     near[0] = cosine
     near[1] = jnp.where(lane < HD // 2, -sine, sine)
 
-    for k in far_first(ny)[::-1]:
-        from_y(k).wait_recv()
+    for k in range(1, ny):
+        pl.when(y >= k)(lambda k=k: from_y(k).wait_recv())
     running = jnp.zeros_like(row_total)
     for j in range(ny):
         running = running + jnp.where(j < y, totals[j].astype(F32), 0.0)
@@ -260,46 +264,61 @@
     def ring_l(s, p):
         return remote(out_l.at[s, p], in_l.at[s, p], rl_send.at[s, p], rl_recv.at[s, p], z=left)
 
-    def pass_r(s, p, first=False):
+    def far_r(p):
+        return remote(far_out.at[p], far_in.at[p], rf_send.at[p], rf_recv.at[p], z=at(2))
+
+    def far_l(p):
+        return remote(far_out.at[p], far_in.at[p], rf_send.at[p], rf_recv.at[p], z=at(-2))
+
+    def pass_far(p):
+        far_out[p] = part[at(half_z), piece_rows[p]].astype(BF)
+        go(far_r(p) if p in early else far_l(p))
+
+    def pass_r(s, p):
         value = part[at(half_z - s), piece_rows[p]]
-        if not first:
+        if s > 1:
             ring_r(s - 1, p).wait_recv()
             value = value + in_r[s - 1, p].astype(F32)
+        if s == half_z - 2 and p in early:
+            far_r(p).wait_recv()
+            value = value + far_in[p].astype(F32)
         out_r[s, p] = value.astype(BF)
         go(ring_r(s, p))
 
-    def pass_l(s, p, first=False):
+    def pass_l(s, p):
         value = part[at(s - half_z), piece_rows[p]]
-        if not first:
+        if s > 1:
             ring_l(s - 1, p).wait_recv()
             value = value + in_l[s - 1, p].astype(F32)
+        if s == half_z - 2 and p in late:
+            far_l(p).wait_recv()
+            value = value + far_in[p].astype(F32)
         out_l[s, p] = value.astype(BF)
         go(ring_l(s, p))
 
     finish_part(half_z)
     for p, q in zip(early, late):
-        pass_r(0, p, True)
-        pass_l(0, q, True)
+        pass_far(p)
+        pass_far(q)
     finish_part(half_z - 1)
-    for q in late:
-        pass_r(1, q, True)
     finish_part(1 - half_z)
-    for p in early:
-        pass_l(1, p, True)
+    for p, q in zip(early, late):
+        pass_r(1, p)
+        pass_l(1, q)
+    for p, q in zip(early, late):
+        pass_r(1, q)
+        pass_l(1, p)
     for k in range(half_z - 2, 0, -1):
         finish_part(k)
         finish_part(-k)
     finish_part(0)
-    for p, q in zip(early, late):
-        pass_r(1, p)
-        pass_l(1, q)
     for s in range(2, half_z):
+        for p, q in zip(early, late):
+            pass_r(s, p)
+            pass_l(s, q)
         for p, q in zip(early, late):
             pass_r(s, q)
             pass_l(s, p)
-        for p, q in zip(early, late):
-            pass_r(s, p)
-            pass_l(s, q)
 
     last = half_z - 1
     acc[...] = jnp.zeros_like(acc)
@@ -313,6 +332,12 @@
 
     def send_l(s, p):
         return remote(piece(s, c, p), piece(s, c, p), gl_send.at[s, p], gl_recv.at[s, p], z=left)
+
+    def jump_r(p):
+        return remote(piece(0, c, p), piece(0, c, p), gr_send.at[1, p], gr_recv.at[1, p], z=at(2))
+
+    def jump_l(p):
+        return remote(piece(0, c, p), piece(0, c, p), gl_send.at[1, p], gl_recv.at[1, p], z=at(-2))
 
     def got_r(s, p):
         here = piece(-s - 1, c, p)
@@ -338,6 +363,7 @@
         mixed = mixed + in_r[last, p].astype(F32) + in_l[last, p].astype(F32)
         mixed = mixed.astype(BF)
         hg[z, c, piece_rows[p]] = mixed
+        go(jump_r(p) if p in early else jump_l(p))
         go(send_r(0, p))
         go(send_l(0, p))
         go(core_copy(0, c, p))
@@ -367,13 +393,13 @@
             for p in (early, late)[h]:
                 got_r(s, p)
                 if h == 0:
-                    send_r(s + 1, p).start()
+                    pl.when(s > 0)(lambda p=p: send_r(s + 1, p).start())
                 else:
                     pl.when(s < last - 1)(lambda p=p: send_r(s + 1, p).start())
                 core_copy(-1 - s, c, p).start()
                 got_l(s, p)
                 if h == 1:
-                    send_l(s + 1, p).start()
+                    pl.when(s > 0)(lambda p=p: send_l(s + 1, p).start())
                 else:
                     pl.when(s < last - 1)(lambda p=p: send_l(s + 1, p).start())
                 core_copy(s + 1, c, p).start()
@@ -385,8 +411,9 @@
 
     lax.fori_loop(0, last, gather_step, 0)
     for s in range(1, half_z):
-        sent += [send_r(s, p) for p in early]
-        sent += [send_l(s, q) for q in late]
+        if s > 1:
+            sent += [send_r(s, p) for p in early]
+            sent += [send_l(s, q) for q in late]
         if s < last:
             sent += [send_r(s, q) for q in late]
             sent += [send_l(s, p) for p in early]
@@ -458,6 +485,8 @@
 
     for copy in sent:
         copy.wait_send()
+    for k in range(1, ny):
+        pl.when(y < ny - k)(lambda k=k: to_y(k).wait_send())
 
 
 def tables(tok, blocks):
@@ -497,6 +526,8 @@
         vmem((half_z, PIECES, tok // PIECES, width), BF),
         vmem((half_z, PIECES, tok // PIECES, width), BF),
         vmem((half_z, PIECES, tok // PIECES, width), BF),
+        vmem((PIECES, tok // PIECES, width), BF),
+        vmem((PIECES, tok // PIECES, width), BF),
         vmem((nz, 2, tok, width), BF),
         vmem((3, tok, width), F32),
         vmem((tok, HD), F32),
@@ -519,6 +550,8 @@
         dma((half_z, PIECES)),
         dma((half_z, PIECES)),
         dma((half_z, PIECES)),
+        dma((PIECES,)),
+        dma((PIECES,)),
         dma((half_z, PIECES)),
         dma((half_z, PIECES)),
         dma((half_z, PIECES)),

time: 81.8 us -> 82.7 us (1.011)
  Pallas kernels: 79.6 us -> 80.5 us
    pallas_call x1, Pallas kernels: 79.6 us -> 80.5 us  [local(): pl.pallas_call(functools.partial(layer_pair, sizes, scale), name='layer_p...]
where the time goes in v3:
time: 82.7 us; the launch traced here: 82.5 us
  Pallas kernels  80.5 us (97%)
  local copies, waits for them, and re-layouts  1.31 us (2%)
    pallas_call x1, Pallas kernels, local(): pl.pallas_call(functools.partial(layer_pair, sizes, scale), name='layer_p...  80.5 us

profile of v3, /device:TPU:1, one launch (start us, length us, event | category | flops | bytes accessed | tf_op | source)
XLA Modules:
  0.0 82.5 jit_solution(9462240870771947187)
XLA Ops:
  0.6 80.5 %layer_pair.1 = (bf16[256,256]{1,0:T(8,128)(2,1)S(1)}, bf16[256,256]{1,0:T(8,128)(2,1)S(1)}) custom-call(bf16[3,256,256]{2,1,0:T(8,128)(2,1)} %bitcast.3, bf16[256,256]{1,0:T(8,128)(2,1)} %resid_hbm.1, bf16[256,4096]{1,0:T(8,128)(2,1)} %wo_hbm.1, bf16[3,4096,256]{2,1,0:T(8,128)(2,1)} %bitcast.2, f32[2,256,128]{2,1,0:T(8,128)} %constant.4.clone.near_hbm, ...), custom_call_target="tpu_custom_call" | custom-call | tf_op jit(solution)/shard_map/layer_pair/pallas_call | solution.py:572
  81.2 0.7 copy.10
  81.8 0.7 copy.11

commit v4 on v3

--- a/solution.py
+++ b/solution.py
@@ -41,8 +41,7 @@
     wq_hbm,
     near_hbm,
     far_hbm,
-    hidden_ref,
-    attended_ref,
+    out_ref,
     qkv,
     resid,
     w2,
@@ -353,72 +352,76 @@
         return remote(here, here, gc_send.at[slot, p], gc_recv.at[slot, p], c=other)
 
     for p in range(PIECES):
-        if p in early:
-            ring_l(last, p).wait_recv()
-            ring_r(last, p).wait_recv()
-        else:
-            ring_r(last, p).wait_recv()
-            ring_l(last, p).wait_recv()
+        ring_r(last, p).wait_recv()
+        ring_l(last, p).wait_recv()
         mixed = resid[piece_rows[p], :].astype(F32) + part[z, piece_rows[p]]
         mixed = mixed + in_r[last, p].astype(F32) + in_l[last, p].astype(F32)
         mixed = mixed.astype(BF)
         hg[z, c, piece_rows[p]] = mixed
-        go(jump_r(p) if p in early else jump_l(p))
+        go(jump_r(p) if p in early else send_r(0, p))
+        go(send_l(0, p) if p in early else jump_l(p))
+        go(core_copy(0, c, p))
+        out_ref[0, piece_rows[p], :] = mixed
+    for p, q in zip(early, late):
         go(send_r(0, p))
-        go(send_l(0, p))
-        go(core_copy(0, c, p))
-        hidden_ref[piece_rows[p], :] = mixed
+        go(send_l(0, q))
     loads[3].wait()
 
-    def project(k, core, h):
+    def project(k, core, rows):
         j = at(k)
-        values = hg[j, core, halves[h]]
+        values = hg[j, core, rows]
         rows_of = pl.ds(pl.multiple_of((2 * j + core) * width, width), width)
         for i in range(3):
-            acc[i, halves[h]] += dot(values, wq[i, rows_of, :])
+            acc[i, rows] += dot(values, wq[i, rows_of, :])
         wide = values.astype(F32)
         squares = wide * wide
-        sumsq[halves[h]] += squares[:, :HD] + squares[:, HD:]
-
-    def project_other(k, h):
-        for p in (early, late)[h]:
+        sumsq[rows] += squares[:, :HD] + squares[:, HD:]
+
+    def project_pair(k, core, rows):
+        def one(i, _):
+            project(k * (1 - 2 * i), core, rows)
+            return 0
+
+        lax.fori_loop(0, 2, one, 0)
+
+    def from_core(k, pieces):
+        for p in pieces:
             core_copy(k, other, p).wait_recv()
-        project(k, other, h)
-
-    project(0, c, 0)
-    project(0, c, 1)
-
-    def gather_step(s, _):
-        for h in range(2):
-            for p in (early, late)[h]:
-                got_r(s, p)
-                if h == 0:
-                    pl.when(s > 0)(lambda p=p: send_r(s + 1, p).start())
-                else:
-                    pl.when(s < last - 1)(lambda p=p: send_r(s + 1, p).start())
-                core_copy(-1 - s, c, p).start()
-                got_l(s, p)
-                if h == 1:
-                    pl.when(s > 0)(lambda p=p: send_l(s + 1, p).start())
-                else:
-                    pl.when(s < last - 1)(lambda p=p: send_l(s + 1, p).start())
-                core_copy(s + 1, c, p).start()
-            project(-1 - s, c, h)
-            project(s + 1, c, h)
-            project_other(-s, h)
-            pl.when(s > 0)(lambda h=h: project_other(s, h))
-        return 0
-
-    lax.fori_loop(0, last, gather_step, 0)
-    for s in range(1, half_z):
-        if s > 1:
-            sent += [send_r(s, p) for p in early]
-            sent += [send_l(s, q) for q in late]
-        if s < last:
-            sent += [send_r(s, q) for q in late]
-            sent += [send_l(s, p) for p in early]
-    for k in range(1, nz):
-        sent += [core_copy(k, c, p) for p in range(PIECES) if k != half_z]
+
+    def take_r(s, pieces, forward):
+        for p in pieces:
+            got_r(s, p)
+            if forward:
+                go(send_r(s + 1, p))
+            go(core_copy(-1 - s, c, p))
+
+    def take_l(s, pieces, forward):
+        for p in pieces:
+            got_l(s, p)
+            if forward:
+                go(send_l(s + 1, p))
+            go(core_copy(s + 1, c, p))
+
+    every, whole = early + late, pl.ds(0, tok)
+    project(0, c, whole)
+    take_r(1, early, True)
+    take_l(0, early, True)
+    take_r(0, late, True)
+    take_l(1, late, True)
+    take_r(0, early, False)
+    take_l(0, late, False)
+    from_core(0, every)
+    project(0, other, whole)
+    project_pair(1, c, whole)
+    for s in range(2, last):
+        take_r(s, early, True)
+        take_l(s - 1, early, True)
+        take_r(s - 1, late, True)
+        take_l(s, late, True)
+        from_core(1 - s, every)
+        from_core(s - 1, every)
+        project_pair(s, c, whole)
+        project_pair(s - 1, other, whole)
 
     def kv_copy(h, i):
         return remote(kv.at[h, i], kvp.at[h, i], kv_send.at[h, i], kv_recv.at[h, i], y=next_y, x=next_x)
@@ -431,17 +434,25 @@
         values = acc[i, halves[h], heads[head]] * scaled
         return (values * near[0, halves[h]] + pltpu.roll(values, HD // 2, 1) * near[1, halves[h]]).astype(BF)
 
+    take_r(last, early, False)
+    take_l(last - 1, early, False)
+    project_pair(last, c, halves[0])
+    project(half_z, c, halves[0])
+    from_core(1 - last, every)
+    from_core(last - 1, every)
+    project_pair(last - 1, other, whole)
+    take_r(last - 1, late, False)
+    take_l(last, late, False)
     for h in range(2):
-        for p in (early, late)[h]:
-            if h == 0:
-                got_r(last, p)
-            else:
-                got_l(last, p)
-            go(core_copy(half_z, c, p))
-        project(half_z, c, h)
-        project_other(-last, h)
-        project_other(last, h)
-        project_other(half_z, h)
+        pieces = (early, late)[h]
+        if h == 1:
+            project_pair(last, c, halves[1])
+            project(half_z, c, halves[1])
+        from_core(-last, pieces)
+        from_core(last, pieces)
+        from_core(half_z, pieces)
+        project_pair(last, other, halves[h])
+        project(half_z, other, halves[h])
         scaled = row_scale(h)
         for head in range(2):
             kv[h, 0, :, heads[head]] = rotated(1, h, head, scaled)
@@ -481,7 +492,7 @@
         for head in range(2):
             outs[head] = outs[head] + dot(weights[head], kvp[h, 1, :, heads[head]])
     for head in range(2):
-        attended_ref[:, heads[head]] = (outs[head] / sums[head]).astype(BF)
+        out_ref[1, :, heads[head]] = (outs[head] / sums[head]).astype(BF)
 
     for copy in sent:
         copy.wait_send()
@@ -569,12 +580,12 @@
         jnp.asarray(near),
         jnp.asarray(far),
     )
-    return pl.pallas_call(
+    both = pl.pallas_call(
         functools.partial(layer_pair, sizes, scale),
         name="layer_pair",
-        out_shape=(jax.ShapeDtypeStruct((tok, width), BF),) * 2,
+        out_shape=jax.ShapeDtypeStruct((2, tok, width), BF),
         in_specs=[anywhere] * 6,
-        out_specs=(pl.BlockSpec(memory_space=pltpu.VMEM),) * 2,
+        out_specs=pl.BlockSpec(memory_space=pltpu.VMEM),
         scratch_shapes=scratch,
         compiler_params=pltpu.CompilerParams(
             collective_id=0, has_side_effects=True, vmem_limit_bytes=48 * 1024 * 1024
@@ -582,6 +593,7 @@
     )(
         *(pltpu.with_memory_space_constraint(array, pltpu.HBM) for array in operands)
     )
+    return both[0], both[1]
 
 
 def on_torus(devices, sizes):

time: 82.7 us -> 80.3 us (0.971)
  Pallas kernels: 80.5 us -> 78.7 us
    pallas_call x1, Pallas kernels: 80.5 us -> 78.7 us  [local(): pl.pallas_call(functools.partial(layer_pair, sizes, scale), name='layer_p...]
    unnamed x2 -> x0, local copies, waits for them, and re-layouts: 1.31 us -> none
where the time goes in v4:
time: 80.3 us; the launch traced here: 80.1 us
  Pallas kernels  78.7 us (98%)
    pallas_call x1, Pallas kernels, local(): pl.pallas_call(functools.partial(layer_pair, sizes, scale), name='layer_p...  78.7 us

profile of v4, /device:TPU:1, one launch (start us, length us, event | category | flops | bytes accessed | tf_op | source)
XLA Modules:
  0.0 80.1 jit_solution(1328565768411901907)
XLA Ops:
  0.6 78.7 %layer_pair.1 = bf16[2,256,256]{2,1,0:T(8,128)(2,1)S(1)} custom-call(bf16[3,256,256]{2,1,0:T(8,128)(2,1)} %bitcast.7, bf16[256,256]{1,0:T(8,128)(2,1)} %resid_hbm.1, bf16[256,4096]{1,0:T(8,128)(2,1)} %wo_hbm.1, bf16[3,4096,256]{2,1,0:T(8,128)(2,1)} %bitcast.6, f32[2,256,128]{2,1,0:T(8,128)} %constant.4.clone.near_hbm, f32[2,64,128]{2,1,0:T(8,128)} %constant.5.clone.far_hbm), custom_call_target="tpu_custom_call" | custom-call | tf_op jit(solution)/shard_map/layer_pair/pallas_call | solution.py:583
  79.4 0.7 slice_bitcast_fusion

commit v5 on v4

--- a/solution.py
+++ b/solution.py
@@ -53,6 +53,9 @@
     totals,
     p3s,
     p3,
+    p3x,
+    qx,
+    locx,
     loc,
     lin2,
     part,
@@ -78,8 +81,12 @@
     r2,
     s3,
     r3,
-    lin_send,
-    lin_recv,
+    s4,
+    r4,
+    qx_send,
+    qx_recv,
+    lx_send,
+    lx_recv,
     rr_send,
     rr_recv,
     rl_send,
@@ -124,6 +131,7 @@
     barrier = pltpu.get_barrier_semaphore()
     greeted = 0
     places = [{"x": lax.rem(x + k, nx)} for k in range(1, nx)]
+    places += [{"x": lax.rem(x + k, nx), "c": other} for k in range(1, nx)]
     places += [{"y": lax.rem(y + k, ny)} for k in range(1, ny)]
     places += [{"z": right}, {"z": left}, {"z": lax.rem(z + 2, nz)}, {"z": lax.rem(z + nz - 2, nz)}, {"c": other}]
     places += [{"y": next_y, "x": next_x}, {"y": prev_y, "x": prev_x}]
@@ -169,6 +177,13 @@
     for load in loads:
         load.start()
 
+    def query_swap():
+        return remote(qkv.at[0], qx, qx_send, qx_recv, c=other)
+
+    def loc_swap():
+        return remote(loc, locx, lx_send, lx_recv, c=other)
+
+    go(query_swap())
     p1[pl.ds(x, 1)] = st[pl.ds(x, 1)]
     rows = lax.broadcasted_iota(jnp.int32, (tok, tok), 0)
     cols = lax.broadcasted_iota(jnp.int32, (tok, tok), 1)
@@ -177,6 +192,7 @@
         scores = dot(qkv[0, :, heads[h]], qkv[1, :, heads[h]], (1, 1))
         inner = jnp.where(causal, scores, 0.0).astype(BF)
         loc[:, heads[h]] = dot(inner, qkv[2, :, heads[h]])
+    go(loc_swap())
 
     for k in far_first(nx)[::-1]:
         from_x(k).wait_recv()
@@ -223,39 +239,44 @@
         there = lax.rem(x + nx - k, nx)
         return remote(p3s.at[there], p3.at[there], s3.at[k], r3.at[k], x=there)
 
+    def cross_x(k):
+        there = lax.rem(x + k, nx)
+        return remote(p3s.at[there], p3x.at[x], s4.at[k], r4.at[k], x=there, c=other)
+
+    def crossed_x(k):
+        there = lax.rem(x + nx - k, nx)
+        return remote(p3s.at[there], p3x.at[there], s4.at[k], r4.at[k], x=there, c=other)
+
     for k in far_first(nx):
         go(back_x(k))
+        go(cross_x(k))
+    go(cross_x(0))
     p3[pl.ds(x, 1)] = p3s[pl.ds(x, 1)]
     for j in range(nz):
         wo_own(j).wait()
         wo_swap(j, other).wait_recv()
     loads[0].wait()
+    query_swap().wait_recv()
+    loc_swap().wait_recv()
+    crossed_x(0).wait_recv()
     for k in far_first(nx)[::-1]:
         got_x(k).wait_recv()
+        crossed_x(k).wait_recv()
 
     for h in range(2):
         before = p3[pl.ds(h * nx // 2, nx // 2)].reshape(HD, HD)
         total = loc[:, heads[h]] + dot(qkv[0, :, heads[h]], before)
         lin2[c, :, heads[h]] = (total * scale).astype(BF)
-
-    def lin_swap(slot):
-        return remote(lin2.at[c], lin2.at[slot], lin_send, lin_recv, c=other)
-
-    go(lin_swap(c))
-
-    def own_part(j, _):
-        part[j] = dot(lin2[c], w2[j, c])
-        return 0
-
-    lax.fori_loop(0, nz, own_part, 0)
-    lin_swap(other).wait_recv()
+        before = p3x[pl.ds(h * nx // 2, nx // 2)].reshape(HD, HD)
+        total = locx[:, heads[h]] + dot(qx[:, heads[h]], before)
+        lin2[other, :, heads[h]] = (total * scale).astype(BF)
 
     def at(k):
         return lax.rem(z + k + nz, nz)
 
     def finish_part(k):
         j = at(k)
-        part[j] = part[j] + dot(lin2[other], w2[j, other])
+        part[j] = dot(lin2[c], w2[j, c]) + dot(lin2[other], w2[j, other])
 
     def ring_r(s, p):
         return remote(out_r.at[s, p], in_r.at[s, p], rr_send.at[s, p], rr_recv.at[s, p], z=right)
@@ -530,6 +551,9 @@
         vmem((ny, rows, HD), BF),
         vmem((nx, rows, HD), BF),
         vmem((nx, rows, HD), BF),
+        vmem((nx, rows, HD), BF),
+        vmem((tok, width), BF),
+        vmem((tok, width), F32),
         vmem((tok, width), F32),
         vmem((2, tok, width), BF),
         vmem((nz, tok, width), F32),
@@ -555,6 +579,10 @@
         dma((ny,)),
         dma((nx,)),
         dma((nx,)),
+        dma((nx,)),
+        dma((nx,)),
+        dma,
+        dma,
         dma,
         dma,
         dma((half_z, PIECES)),

time: 80.3 us -> 79.9 us (level)
  no operation moved by 1% of the time
where the time goes in v5:
time: 79.9 us; the launch traced here: 79.7 us
  Pallas kernels  78.4 us (98%)
    pallas_call x1, Pallas kernels, local(): pl.pallas_call(functools.partial(layer_pair, sizes, scale), name='layer_p...  78.4 us

profile of v5, /device:TPU:1, one launch (start us, length us, event | category | flops | bytes accessed | tf_op | source)
XLA Modules:
  0.0 79.7 jit_solution(15558227528359364293)
XLA Ops:
  0.6 78.4 %layer_pair.1 = bf16[2,256,256]{2,1,0:T(8,128)(2,1)S(1)} custom-call(bf16[3,256,256]{2,1,0:T(8,128)(2,1)} %bitcast.7, bf16[256,256]{1,0:T(8,128)(2,1)} %resid_hbm.1, bf16[256,4096]{1,0:T(8,128)(2,1)} %wo_hbm.1, bf16[3,4096,256]{2,1,0:T(8,128)(2,1)} %bitcast.6, f32[2,256,128]{2,1,0:T(8,128)} %constant.4.clone.near_hbm, f32[2,64,128]{2,1,0:T(8,128)} %constant.5.clone.far_hbm), custom_call_target="tpu_custom_call" | custom-call | tf_op jit(solution)/shard_map/layer_pair/pallas_call | solution.py:611
  79.0 0.7 slice_bitcast_fusion

commit v6 on v5

--- a/solution.py
+++ b/solution.py
@@ -333,11 +333,8 @@
         finish_part(-k)
     finish_part(0)
     for s in range(2, half_z):
-        for p, q in zip(early, late):
+        for p in early + late:
             pass_r(s, p)
-            pass_l(s, q)
-        for p, q in zip(early, late):
-            pass_r(s, q)
             pass_l(s, p)
 
     last = half_z - 1

time: 79.9 us -> 79.6 us (level)
  no operation moved by 1% of the time
where the time goes in v6:
time: 79.6 us; the launch traced here: 79.5 us
  Pallas kernels  78.1 us (98%)
    pallas_call x1, Pallas kernels, local(): pl.pallas_call(functools.partial(layer_pair, sizes, scale), name='layer_p...  78.1 us

profile of v6, /device:TPU:1, one launch (start us, length us, event | category | flops | bytes accessed | tf_op | source)
XLA Modules:
  0.0 79.5 jit_solution(14853516715394844326)
XLA Ops:
  0.6 78.1 %layer_pair.1 = bf16[2,256,256]{2,1,0:T(8,128)(2,1)S(1)} custom-call(bf16[3,256,256]{2,1,0:T(8,128)(2,1)} %bitcast.7, bf16[256,256]{1,0:T(8,128)(2,1)} %resid_hbm.1, bf16[256,4096]{1,0:T(8,128)(2,1)} %wo_hbm.1, bf16[3,4096,256]{2,1,0:T(8,128)(2,1)} %bitcast.6, f32[2,256,128]{2,1,0:T(8,128)} %constant.4.clone.near_hbm, f32[2,64,128]{2,1,0:T(8,128)} %constant.5.clone.far_hbm), custom_call_target="tpu_custom_call" | custom-call | tf_op jit(solution)/shard_map/layer_pair/pallas_call | solution.py:608
  78.7 0.7 slice_bitcast_fusion
